TPU v7x, 256 devices: a whole 4x4x8 slice. The times are simulated.
256 devices in a mesh: space: 32 (over y_hi, z, core), coil: 8 (over y_lo, x).
Axes of the slice: x: 4, y: 4 (y_hi: 2, y_lo: 2; y = y_hi * 2 + y_lo), z: 8, core: 2. Of those that a mesh axis runs over, the one named last changes fastest.
Arguments:
- spatial_coef: bfloat16 [16, 128, 128, 2, 128], P('coil', 'space'), may hold values from -6 to 6
- temporal_basis: bfloat16 [2, 16, 4], replicated, may hold values from -1.5 to 1.5
- coil_maps: bfloat16 [32, 128, 128, 2, 128], P('coil', 'space'), may hold values from -6 to 6
- field_steps: int32 [128, 128, 128], P('space'), may hold values from 0 to 255
- kspace_data: bfloat16 [32, 4, 128, 128, 2, 128], P('coil', None, None, 'space'), may hold values from -6 to 6
- sample_mask: int32 [4, 128, 128], P(None, 'space'), may hold values 0 or 1
Outputs:
- gradient: float32 [16, 128, 128, 2, 128], P('coil', 'space')
Inputs may be any that keep to these rules, and one draw needn't show every extreme that they name: `sample_mask`: 1 where a phase-encoding line is sampled at that point, else 0.
All inputs are finite; a program needn't handle non-finite values. No bound on the sum of `sample_mask` on one device may be relied on, other than what follows from the above.
Results may differ from a plain program's by a relative error of at most 0.014.
Values may be sent and summed in bfloat16 or wider, within the bound.
A program may use at most 64 MiB of HBM per device.

v0:
```python
import math
import jax
import jax.numpy as jnp
from jax import lax
from jax.sharding import PartitionSpec as P

STEPS_CYCLE = 256


def dft_table(length, sign):
    index = jnp.arange(length, dtype=jnp.int32)
    steps = index[:, None] * index[None, :] % length
    angle = steps.astype(jnp.float32) * (2.0 * math.pi / length)
    scale = 1.0 / math.sqrt(length)
    cosine = jnp.cos(angle) * scale
    sine = jnp.sin(angle) * (sign * scale)
    upper = jnp.stack([cosine, sine], axis=1)
    lower = jnp.stack([-sine, cosine], axis=1)
    return jnp.stack([upper, lower], axis=0).astype(jnp.bfloat16)


def forward_mix(basis):
    real_part = basis[0]
    imaginary = basis[1]
    return jnp.stack(
        [jnp.stack([real_part, imaginary], -1), jnp.stack([-imaginary, real_part], -1)], 1
    )


def adjoint_mix(basis):
    real_part = basis[0].T
    imaginary = basis[1].T
    return jnp.stack(
        [jnp.stack([real_part, -imaginary], -1), jnp.stack([imaginary, real_part], -1)], 1
    )


def phase_parts(field_steps, points):
    counter = jnp.arange(1, points + 1, dtype=jnp.int32)
    steps = field_steps[None] * counter[:, None, None, None] % STEPS_CYCLE
    angle = steps.astype(jnp.float32) * (2.0 * math.pi / STEPS_CYCLE)
    return (jnp.cos(angle), jnp.sin(angle))


def transform(volume, table, form):
    return jnp.einsum(form, volume, table, preferred_element_type=jnp.float32)


def shards(spatial_coef, temporal_basis, coil_maps, field_steps, kspace_data, sample_mask):
    points = temporal_basis.shape[2]
    section = temporal_basis
    data_first = transform(
        kspace_data, dft_table(kspace_data.shape[2], 1.0), "ctxypz,pxqk->ctkyqz"
    ).astype(jnp.bfloat16)
    measured = lax.all_to_all(data_first, "space", split_axis=2, concat_axis=3, tiled=True)
    mask_all = lax.all_gather(sample_mask.astype(jnp.bfloat16), "space", axis=1, tiled=True)
    mask_all = mask_all.astype(jnp.float32)[None, :, None, :, None, :]
    image = jnp.einsum(
        "lxypz,lptq->txyqz",
        lax.all_gather(spatial_coef, "coil", axis=0, tiled=True),
        forward_mix(section),
        preferred_element_type=jnp.float32,
    )
    cosine, sine = phase_parts(field_steps, points)
    image_real = image[:, :, :, 0]
    image_imaginary = image[:, :, :, 1]
    turned_real = cosine * image_real - sine * image_imaginary
    turned_imaginary = sine * image_real + cosine * image_imaginary
    map_real = coil_maps[:, :, :, 0].astype(jnp.float32)[:, None]
    map_imaginary = coil_maps[:, :, :, 1].astype(jnp.float32)[:, None]
    coil_real = map_real * turned_real - map_imaginary * turned_imaginary
    coil_imaginary = map_real * turned_imaginary + map_imaginary * turned_real
    coil_image = jnp.stack([coil_real, coil_imaginary], axis=4).astype(jnp.bfloat16)
    depth_count = coil_image.shape[5]
    row_count = coil_image.shape[3]
    depth_pass = transform(coil_image, dft_table(depth_count, -1.0), "ctxypz,pzqk->ctxyqk").astype(
        jnp.bfloat16
    )
    row_pass = transform(depth_pass, dft_table(row_count, -1.0), "ctxypz,pyqk->ctxkqz")
    residual = (mask_all * (row_pass - measured.astype(jnp.float32))).astype(jnp.bfloat16)
    back_rows = transform(residual, dft_table(row_count, 1.0), "ctxypz,pyqk->ctxkqz").astype(
        jnp.bfloat16
    )
    back_image = transform(back_rows, dft_table(depth_count, 1.0), "ctxypz,pzqk->ctxyqk")
    back_real = back_image[:, :, :, :, 0]
    back_imaginary = back_image[:, :, :, :, 1]
    sum_real = jnp.sum(map_real * back_real + map_imaginary * back_imaginary, axis=0)
    sum_imaginary = jnp.sum(map_real * back_imaginary - map_imaginary * back_real, axis=0)
    combined_real = cosine * sum_real + sine * sum_imaginary
    combined_imaginary = cosine * sum_imaginary - sine * sum_real
    combined = jnp.stack([combined_real, combined_imaginary], axis=3)
    section = temporal_basis.astype(jnp.float32)
    return lax.psum_scatter(
        jnp.einsum(
            "txypz,tplq->lxyqz", combined, adjoint_mix(section), precision=lax.Precision.HIGHEST
        ).astype(jnp.bfloat16),
        "coil",
        scatter_dimension=0,
        tiled=True,
    ).astype(jnp.float32)


def solution(mesh):
    in_specs = (
        P("coil", "space", None, None, None),
        P(),
        P("coil", "space", None, None, None),
        P("space", None, None),
        P("coil", None, None, "space", None, None),
        P(None, "space", None),
    )
    out_specs = P("coil", "space", None, None, None)
    return jax.shard_map(shards, mesh=mesh, in_specs=in_specs, out_specs=out_specs, check_vma=False)
```

profile of v0, /device:TPU:1, one launch (start us, length us, event | category | flops | bytes accessed | tf_op | source)
XLA Modules:
  0.0 291.8 jit_solution(16822251822179773445)
XLA Ops:
  6.5 0.0 all-gather.2.cloned.1.call-start
  6.5 1.9 copy.62
  8.5 0.0 all-gather.2.cloned.1.call-update
  8.5 0.3 negate_convert_fusion
  8.8 0.3 multiply_convert_fusion
  9.1 0.3 multiply_convert_fusion.2
  9.3 0.7 fusion.59
  10.0 3.5 %fusion.5 = bf16[4,4,128,4,2,128]{5,2,3,1,0,4:T(8,128)(2,1)S(1)} fusion(bf16[4,4,128,4,2,128]{5,4,3,2,1,0:T(2,128)(2,1)} %param.10, bf16[1,128,2,128]{3,1,2,0:T(8,128)(2,1)S(1)} %get-tuple-element.17, bf16[1,128,2,128]{3,1,2,0:T(8,128)(2,1)S(1)} %get-tuple-element.18), kind=kOutput, calls=%fused_computation.9 | convolution fusion | flops 1075904512 | bytes 8519680 | tf_op jit(solution)/shard_map/ctxypz,pxqk->ctkyqz/dot_general | solution.py:46
  13.5 5.2 %copy.68 = bf16[4,4,128,4,2,128]{5,3,1,0,4,2:T(4,128)(2,1)} copy(bf16[4,4,128,4,2,128]{5,2,3,1,0,4:T(8,128)(2,1)S(1)} %fusion.5) | data formatting | bytes 8388608 | tf_op jit(solution)/shard_map/convert_element_type | solution.py:54
  18.7 0.0 copy-start.4
  18.7 0.0 copy-start.5
  18.7 0.0 copy-start
  18.7 12.9 %all-to-all-start = ((bf16[4,4,128,4,2,128]{5,3,1,0,4,2:T(4,128)(2,1)}), bf16[4,4,128,4,2,128]{5,3,1,0,4,2:T(4,128)(2,1)}, u32[]{:S(2)}, u32[]{:S(2)}) async-start(bf16[4,4,128,4,2,128]{5,3,1,0,4,2:T(4,128)(2,1)} %copy.68), calls=%async_computation | async-start | bytes 8388608 | tf_op jit(solution)/shard_map/all_to_all | solution.py:55
  31.7 0.0 reduce-scatter.2.cloned.1.call-start
  31.7 0.0 copy-done.4
  31.8 0.0 copy-done.5
  31.8 135.0 %all_gather.6 = bf16[4,128,128]{2,0,1:T(4,128)(2,1)S(1)} all-gather(bf16[4,4,128]{2,0,1:T(4,128)(2,1)S(1)} %copy_convert_fusion.1), channel_id=1, replica_groups=mesh['space'=32,'coil'=8] {'space'}, dimensions={1}, use_global_device_ids=true | all-gather | bytes 135168 | tf_op jit(solution)/shard_map/all_gather | solution.py:56
  166.8 0.5 iota_add_fusion
  167.4 0.0 copy-done
  167.4 2.2 slice_convert_fusion.1
  169.6 0.0 all-gather.2.cloned.1.call-done
  169.6 0.0 copy-start.1
  169.6 0.0 copy-start.6
  169.7 4.9 %fusion.36 = f32[4,2,4,128,128]{4,0,3,2,1:T(4,128)S(1)} fusion(bf16[16,4,128,2,128]{4,2,3,1,0:T(8,128)(2,1)} %all-gather.2.cloned.1.call-done, bf16[16,1,4,2]{0,2,1,3:T(4,128)(2,1)S(1)} %get-tuple-element.26, bf16[16,1,4,2]{0,2,1,3:T(4,128)(2,1)S(1)} %get-tuple-element.25), kind=kOutput, calls=%fused_computation.43 | convolution fusion | flops 33555456 | bytes 6291968 | tf_op jit(solution)/shard_map/lxypz,lptq->txyqz/dot_general | solution.py:58
  174.5 0.3 copy.124
  174.8 0.0 copy-done.1
  174.8 0.0 copy-done.6
  174.8 4.6 %multiply_subtract_fusion = (f32[4,4,128,128]{3,2,1,0:T(8,128)S(1)}, f32[4,4,128,128]{3,2,1,0:T(8,128)S(1)}) fusion(f32[4,4,128,2,128]{4,2,1,0,3:T(8,128)S(1)} %bitcast.236, s32[4]{0:T(128)S(1)} %copy-done.6, s32[4,128,128]{2,1,0:T(8,128)S(1)} %copy-done.1), kind=kLoop, calls=%fused_computation.64 | loop fusion | flops 5242880 | bytes 4456464 | tf_op jit(solution)/shard_map/sub | solution.py:67
  179.4 0.0 copy-start.2
  179.4 0.0 copy-start.3
  179.5 3.1 %subtract_convert_fusion = (bf16[4,4,4,128,1,128]{5,3,4,2,1,0:T(8,128)(2,1)}, bf16[4,4,4,128,1,128]{5,3,4,2,1,0:T(8,128)(2,1)}) fusion(f32[4,4,128,128]{3,2,1,0:T(8,128)S(1)} %get-tuple-element.12, f32[4,4,128,128]{3,2,1,0:T(8,128)S(1)} %bitcast.234, f32[4,4,128,128]{3,2,1,0:T(8,128)S(1)} %get-tuple-element.11, f32[4,4,128,128]{3,2,1,0:T(8,128)S(1)} %bitcast.232), kind=kLoop, calls=%fused_computation.30 | loop fusion | flops 8388608 | bytes 8388608 | tf_op jit(solution)/shard_map/convert.5
  182.5 0.0 copy-done.2
  182.5 0.0 copy-done.3
  182.5 8.0 %fusion.3 = f32[2,128,4,4,4,128,1]{5,1,6,0,4,3,2:T(8,128)} fusion(bf16[4,4,4,128,1,128]{5,3,4,2,1,0:T(8,128)(2,1)} %get-tuple-element.8, bf16[4,4,4,128,1,128]{5,3,4,2,1,0:T(8,128)(2,1)} %get-tuple-element.7, bf16[1,128,2,128]{3,1,0,2:T(8,128)(2,1)S(1)} %copy-done.3, bf16[1,128,2,128]{3,1,0,2:T(8,128)(2,1)S(1)} %copy-done.2), kind=kOutput, calls=%fused_computation.8 | convolution fusion | flops 2158493696 | bytes 12713984 | tf_op jit(solution)/shard_map/ctxypz,pyqk->ctxkqz/dot_general | solution.py:46
  190.5 0.0 all-to-all-done
  190.5 7.6 %copy.69 = f32[4,4,32,4,4,2,128]{6,4,2,5,3,1,0:T(4,128)} copy(bf16[4,4,32,4,4,2,128]{6,4,1,0,5,3,2:T(4,128)(2,1)} %bitcast.88) | data formatting | bytes 12582912 | tf_op jit(solution)/shard_map/convert_element_type | solution.py:80
  198.1 11.5 %fusion.27 = f32[4,4,4,128,2,128]{5,3,4,2,1,0:T(8,128)} fusion(f32[4,4,4,128,2,128]{5,3,4,2,1,0:T(8,128)} %bitcast.231, f32[2,128,4,4,4,128,1]{5,1,6,0,4,3,2:T(8,128)} %fusion.3, f32[4,128,128]{2,1,0:T(8,128)S(1)} %copy_convert_fusion, bf16[1,128,2,128]{3,1,2,0:T(8,128)(2,1)S(1)} %get-tuple-element.17, bf16[1,128,2,128]{3,1,2,0:T(8,128)(2,1)S(1)} %get-tuple-element.18), kind=kOutput, calls=%fused_computation.32 | convolution fusion | flops 2156396544 | bytes 25559040 | tf_op jit(solution)/shard_map/ctxypz,pzqk->ctxyqk/dot_general | solution.py:46
  209.6 4.3 %add_reduce_fusion = (f32[4,4,128,128]{3,2,1,0:T(8,128)S(1)}, f32[4,4,128,128]{3,2,1,0:T(8,128)S(1)}) fusion(f32[4,4,4,128,2,128]{5,3,4,2,1,0:T(8,128)} %fusion.27, f32[4,4,128,128]{3,2,1,0:T(8,128)S(1)} %bitcast.235, f32[4,4,128,128]{3,2,1,0:T(8,128)S(1)} %bitcast.233), kind=kLoop, calls=%fused_computation.28 | loop fusion | flops 7864320 | bytes 12582912 | tf_op jit(solution)/shard_map/reduce_sum | solution.py:87
  213.9 9.6 %fusion.45 = (f32[4,4,128,1,128]{4,0,3,2,1:T(4,128)S(1)}, f32[4,4,128,1,128]{4,0,3,2,1:T(4,128)S(1)}) fusion(f32[4,4,128,128]{3,2,1,0:T(8,128)S(1)} %get-tuple-element.6, f32[4,4,128,128]{3,2,1,0:T(8,128)S(1)} %get-tuple-element.5, s32[4]{0:T(128)S(1)} %copy-done.6, s32[4,128,128]{2,1,0:T(8,128)S(1)} %copy-done.1), kind=kLoop, calls=%fused_computation.58 | loop fusion | flops 5242880 | bytes 4456464 | tf_op jit(solution)/shard_map/add | solution.py:89
  223.6 8.0 %fusion.6 = bf16[16,4,128,2,128]{4,0,2,1,3:T(8,128)(2,1)S(1)} fusion(f32[4,4,128,1,128]{4,0,3,2,1:T(4,128)S(1)} %get-tuple-element.10, f32[4,4,128,1,128]{4,0,3,2,1:T(4,128)S(1)} %get-tuple-element.9, f32[4,1,16,2]{2,0,1,3:T(4,128)S(1)} %get-tuple-element.22, f32[4,1,16,2]{2,0,1,3:T(4,128)S(1)} %get-tuple-element.21), kind=kOutput, calls=%fused_computation.10 | convolution fusion | flops 203948288 | bytes 6292480 | tf_op jit(solution)/shard_map/txypz,tplq->lxyqz/dot_general | solution.py:94
  231.6 3.1 %copy.75 = bf16[16,4,128,2,128]{4,2,3,1,0:T(8,128)(2,1)} copy(bf16[16,4,128,2,128]{4,0,2,1,3:T(8,128)(2,1)S(1)} %fusion.6) | data formatting | bytes 8388608 | tf_op jit(solution)/shard_map/convert_element_type | solution.py:96
  234.6 0.0 reduce-scatter.2.cloned.1.call-update
  234.7 47.7 %reduce-scatter.2.cloned.1.call-done = bf16[2,4,128,2,128]{4,2,3,1,0:T(8,128)(2,1)} async-done(((bf16[16,4,128,2,128]{4,2,3,1,0:T(8,128)(2,1)}), bf16[2,4,128,2,128]{4,2,3,1,0:T(8,128)(2,1)}) %reduce-scatter.2.cloned.1.call-update) | async-done | bytes 524304 | tf_op jit(solution)/shard_map/reduce_scatter | solution.py:93
  282.4 2.6 copy.76
  (9 shorter events, 0.1 us)
Async XLA Ops:
  6.5 163.1 %all-gather.2.cloned.1.call-start = ((), (), s32[]{:S(2)}) async-start(), calls=%async_computation.2 | async-start | bytes 4718592 | tf_op jit(solution)/shard_map/all_gather | solution.py:60
  18.7 13.0 %copy-start.4 = (bf16[2,16,4]{1,2,0:T(4,128)(2,1)S(1)}, bf16[2,16,4]{1,2,0:T(4,128)(2,1)}, u32[]{:S(2)}) copy-start(bf16[2,16,4]{1,2,0:T(4,128)(2,1)} %param.7) | copy-start | bytes 772
  18.7 13.0 %copy-start.5 = (s32[4,4,128]{2,1,0:T(4,128)S(1)}, s32[4,4,128]{2,1,0:T(4,128)}, u32[]{:S(2)}) copy-start(s32[4,4,128]{2,1,0:T(4,128)} %param.11) | copy-start | bytes 24580
  18.7 148.7 %copy-start = (bf16[4,4,128,2,128]{4,3,2,1,0:T(2,128)(2,1)S(1)}, bf16[4,4,128,2,128]{4,3,2,1,0:T(2,128)(2,1)}, u32[]{:S(2)}) copy-start(bf16[4,4,128,2,128]{4,3,2,1,0:T(2,128)(2,1)} %param.8) | copy-start | bytes 3145732
  18.7 171.8 %all-to-all-start = ((bf16[4,4,128,4,2,128]{5,3,1,0,4,2:T(4,128)(2,1)}), bf16[4,4,128,4,2,128]{5,3,1,0,4,2:T(4,128)(2,1)}, u32[]{:S(2)}, u32[]{:S(2)}) async-start(bf16[4,4,128,4,2,128]{5,3,1,0,4,2:T(4,128)(2,1)} %copy.68), calls=%async_computation | async-start | bytes 8388608 | tf_op jit(solution)/shard_map/all_to_all | solution.py:55
  31.7 250.7 %reduce-scatter.2.cloned.1.call-start = ((), (), s32[]{:S(2)}) async-start(), calls=%async_computation.3 | async-start | bytes 4718592 | tf_op jit(solution)/shard_map/reduce_scatter | solution.py:93
  169.6 5.2 %copy-start.1 = (s32[4,128,128]{2,1,0:T(8,128)S(1)}, s32[4,128,128]{2,1,0:T(8,128)}, u32[]{:S(2)}) copy-start(s32[4,128,128]{2,1,0:T(8,128)} %param.9) | copy-start | bytes 786436
  169.6 5.1 %copy-start.6 = (s32[4]{0:T(128)S(1)}, s32[4]{0:T(128)}, u32[]{:S(2)}) copy-start(s32[4]{0:T(128)} %iota_add_fusion) | copy-start | bytes 52
  179.4 3.1 %copy-start.2 = (bf16[1,128,2,128]{3,1,0,2:T(8,128)(2,1)S(1)}, bf16[1,128,2,128]{3,1,0,2:T(8,128)(2,1)}, u32[]{:S(2)}) copy-start(bf16[1,128,2,128]{3,1,0,2:T(8,128)(2,1)} %get-tuple-element.15) | copy-start | bytes 196612
  179.4 3.1 %copy-start.3 = (bf16[1,128,2,128]{3,1,0,2:T(8,128)(2,1)S(1)}, bf16[1,128,2,128]{3,1,0,2:T(8,128)(2,1)}, u32[]{:S(2)}) copy-start(bf16[1,128,2,128]{3,1,0,2:T(8,128)(2,1)} %get-tuple-element.16) | copy-start | bytes 196612
Sparse Core Ops, SparseCore 0:
  9.1 79.6 all-gather.1
  234.8 47.5 reduce-scatter.1
where the time goes:
time: 292 us
  blocking collectives  135 us (46%)
  waiting for transfers between devices  47.8 us (16%)
  matrix products  35.8 us (12%)
  other arithmetic  26 us (9%)
  local copies, waits for them, and re-layouts  20.6 us (7%)
  between operations  13.6 us (5%)
  starting transfers between devices  13 us (4%)
    all_gather x1, blocking collectives, shards(): lax.all_gather(sample_mask.astype(jnp.bfloat16), 'space', axis=1, tiled=T...  135 us
    reduce_scatter x1, waiting for transfers between devices, shards(): lax.psum_scatter(jnp.einsum('txypz,tplq->lxyqz', combined, adjoint_mix(se...  47.7 us
    dot_general x3, matrix products, transform(): return jnp.einsum(form, volume, table, preferred_element_type=jnp.float32)  23 us
    all_to_all x1, starting transfers between devices, shards(): lax.all_to_all(data_first, 'space', split_axis=2, concat_axis=3, tiled=True)  12.9 us
    add x1, other arithmetic, shards(): combined_real = cosine * sum_real + sine * sum_imaginary  9.64 us
    dot_general x1, matrix products, shards(): jnp.einsum('txypz,tplq->lxyqz', combined, adjoint_mix(section), precision...  7.99 us
    convert_element_type x1, local copies, waits for them, and re-layouts, shards(): measured.astype(jnp.float32)  7.58 us
  transfers between devices with their start and end apart: 3, of which 1 were waited for; matrix products, arithmetic and copies ran while one was open for 12% of the time, Pallas kernels for 0%

commit v1 on v0

--- a/solution.py
+++ b/solution.py
@@ -53,7 +53,12 @@
         kspace_data, dft_table(kspace_data.shape[2], 1.0), "ctxypz,pxqk->ctkyqz"
     ).astype(jnp.bfloat16)
     measured = lax.all_to_all(data_first, "space", split_axis=2, concat_axis=3, tiled=True)
-    mask_all = lax.all_gather(sample_mask.astype(jnp.bfloat16), "space", axis=1, tiled=True)
+    mask_all = jnp.concatenate(
+        lax.all_to_all(
+            jnp.stack([sample_mask.astype(jnp.bfloat16)] * lax.axis_size("space")), "space", 0, 0
+        ),
+        axis=1,
+    )
     mask_all = mask_all.astype(jnp.float32)[None, :, None, :, None, :]
     image = jnp.einsum(
         "lxypz,lptq->txyqz",

time: 292 us -> 255 us (0.87)
  blocking collectives: 135 us -> 0 us
  waiting for transfers between devices: 47.8 us -> 136 us
  starting transfers between devices: 13 us -> 21.6 us
    all_gather x1 -> x0, blocking collectives: 135 us -> none  [shards(): lax.all_gather(sample_mask.astype(jnp.bfloat16), 'space', axis=1, tiled=T...]
    all_to_all x1, waiting for transfers between devices: 0.01 us -> 35.9 us  [shards(): lax.all_to_all(data_first, 'space', split_axis=2, concat_axis=3, tiled=True)]
    all_gather x1, waiting for transfers between devices: 0.02 us -> 35.4 us  [shards(): lax.all_gather(spatial_coef, 'coil', axis=0, tiled=True)]
    reduce_scatter x1, waiting for transfers between devices: 47.7 us -> 63.4 us  [shards(): lax.psum_scatter(jnp.einsum('txypz,tplq->lxyqz', combined, adjoint_mix(se...]
    all_to_all x0 -> x1, starting transfers between devices: none -> 12.8 us  [shards(): lax.all_to_all(jnp.stack([sample_mask.astype(jnp.bfloat16)] * lax.axis_si...]
    all_to_all x1, starting transfers between devices: 12.9 us -> 8.82 us  [shards(): lax.all_to_all(data_first, 'space', split_axis=2, concat_axis=3, tiled=True)]
  transfers between devices with their start and end apart: 3 -> 4, of which waited for: 1 -> 4; matrix products, arithmetic and copies ran while one was open for 12% -> 14% of each run, Pallas kernels for 0% -> 0%
where the time goes in v1:
time: 255 us; the launch traced here: 254 us
  waiting for transfers between devices  136 us (53%)
  matrix products  36 us (14%)
  other arithmetic  26 us (10%)
  starting transfers between devices  21.6 us (8%)
  local copies, waits for them, and re-layouts  21.4 us (8%)
  between operations  13.6 us (5%)
    reduce_scatter x1, waiting for transfers between devices, shards(): lax.psum_scatter(jnp.einsum('txypz,tplq->lxyqz', combined, adjoint_mix(se...  63.4 us
    all_to_all x1, waiting for transfers between devices, shards(): lax.all_to_all(data_first, 'space', split_axis=2, concat_axis=3, tiled=True)  35.9 us
    all_gather x1, waiting for transfers between devices, shards(): lax.all_gather(spatial_coef, 'coil', axis=0, tiled=True)  35.4 us
    dot_general x3, matrix products, transform(): return jnp.einsum(form, volume, table, preferred_element_type=jnp.float32)  23.1 us
    all_to_all x1, starting transfers between devices, shards(): lax.all_to_all(jnp.stack([sample_mask.astype(jnp.bfloat16)] * lax.axis_si...  12.8 us
    add x1, other arithmetic, shards(): combined_real = cosine * sum_real + sine * sum_imaginary  9.64 us
    all_to_all x1, starting transfers between devices, shards(): lax.all_to_all(data_first, 'space', split_axis=2, concat_axis=3, tiled=True)  8.82 us
    dot_general x1, matrix products, shards(): jnp.einsum('txypz,tplq->lxyqz', combined, adjoint_mix(section), precision...  7.98 us
  transfers between devices with their start and end apart: 4, of which 4 were waited for; matrix products, arithmetic and copies ran while one was open for 14% of the time, Pallas kernels for 0%

profile of v1, /device:TPU:1, one launch (start us, length us, event | category | flops | bytes accessed | tf_op | source)
XLA Modules:
  0.0 254.3 jit_solution(9410371731216587550)
XLA Ops:
  6.5 0.0 all-gather.2.cloned.1.call-start
  6.5 1.9 copy.60
  8.5 0.0 all-gather.2.cloned.1.call-update
  8.5 0.7 convert_element_type.156
  9.2 0.7 stack.76
  9.9 12.8 %all-to-all-start = ((bf16[32,4,4,128]{3,2,1,0:T(4,128)(2,1)}), bf16[32,4,4,128]{3,2,1,0:T(4,128)(2,1)S(1)}, u32[]{:S(2)}, u32[]{:S(2)}) async-start(bf16[32,4,4,128]{3,2,1,0:T(4,128)(2,1)} %stack.76), calls=%async_computation | async-start | bytes 262144 | tf_op jit(solution)/shard_map/all_to_all | solution.py:57
  22.7 0.3 negate_convert_fusion
  22.9 0.3 multiply_convert_fusion
  23.2 0.3 multiply_convert_fusion.2
  23.5 3.7 %fusion.5 = bf16[4,4,128,4,2,128]{5,2,3,1,0,4:T(8,128)(2,1)S(1)} fusion(bf16[4,4,128,4,2,128]{5,4,3,2,1,0:T(2,128)(2,1)} %param.10, bf16[1,128,2,128]{3,1,2,0:T(8,128)(2,1)S(1)} %get-tuple-element.17, bf16[1,128,2,128]{3,1,2,0:T(8,128)(2,1)S(1)} %get-tuple-element.18), kind=kOutput, calls=%fused_computation.9 | convolution fusion | flops 1075904512 | bytes 8519680 | tf_op jit(solution)/shard_map/ctxypz,pxqk->ctkyqz/dot_general | solution.py:46
  27.2 5.2 %copy.66 = bf16[4,4,128,4,2,128]{5,3,1,0,4,2:T(4,128)(2,1)} copy(bf16[4,4,128,4,2,128]{5,2,3,1,0,4:T(8,128)(2,1)S(1)} %fusion.5) | data formatting | bytes 8388608 | tf_op jit(solution)/shard_map/convert_element_type | solution.py:54
  32.4 0.0 copy-start.2
  32.4 0.0 copy-start
  32.4 1.2 all-to-all-done
  33.6 8.8 %all-to-all-start.1 = ((bf16[4,4,128,4,2,128]{5,3,1,0,4,2:T(4,128)(2,1)}), bf16[4,4,128,4,2,128]{5,3,1,0,4,2:T(4,128)(2,1)}, u32[]{:S(2)}, u32[]{:S(2)}) async-start(bf16[4,4,128,4,2,128]{5,3,1,0,4,2:T(4,128)(2,1)} %copy.66), calls=%async_computation.1 | async-start | bytes 8388608 | tf_op jit(solution)/shard_map/all_to_all | solution.py:55
  42.4 0.0 reduce-scatter.2.cloned.1.call-start
  42.5 0.0 copy-done.2
  42.5 0.5 iota_add_fusion
  43.0 0.0 copy-done
  43.0 2.2 slice_convert_fusion.1
  45.3 35.4 %all-gather.2.cloned.1.call-done = bf16[16,4,128,2,128]{4,2,3,1,0:T(8,128)(2,1)} async-done(((bf16[2,4,128,2,128]{4,2,3,1,0:T(8,128)(2,1)}), bf16[16,4,128,2,128]{4,2,3,1,0:T(8,128)(2,1)}) %all-gather.2.cloned.1.call-update) | async-done | bytes 4194320 | tf_op jit(solution)/shard_map/all_gather | solution.py:65
  80.7 0.0 copy-start.1
  80.7 0.0 copy-start.3
  80.7 4.9 %fusion.36 = f32[4,2,4,128,128]{4,0,3,2,1:T(4,128)S(1)} fusion(bf16[16,4,128,2,128]{4,2,3,1,0:T(8,128)(2,1)} %all-gather.2.cloned.1.call-done, bf16[16,1,4,2]{0,2,1,3:T(4,128)(2,1)S(1)} %get-tuple-element.26, bf16[16,1,4,2]{0,2,1,3:T(4,128)(2,1)S(1)} %get-tuple-element.25), kind=kOutput, calls=%fused_computation.43 | convolution fusion | flops 33555456 | bytes 6291968 | tf_op jit(solution)/shard_map/lxypz,lptq->txyqz/dot_general | solution.py:63
  85.6 0.3 copy.120
  85.8 0.0 copy-done.1
  85.8 0.0 copy-done.3
  85.9 4.6 %multiply_subtract_fusion = (f32[4,4,128,128]{3,2,1,0:T(8,128)S(1)}, f32[4,4,128,128]{3,2,1,0:T(8,128)S(1)}) fusion(f32[4,4,128,2,128]{4,2,1,0,3:T(8,128)S(1)} %bitcast.239, s32[4]{0:T(128)S(1)} %copy-done.3, s32[4,128,128]{2,1,0:T(8,128)S(1)} %copy-done.1), kind=kLoop, calls=%fused_computation.64 | loop fusion | flops 5242880 | bytes 4456464 | tf_op jit(solution)/shard_map/sub | solution.py:72
  90.5 3.1 %subtract_convert_fusion = (bf16[4,4,4,128,1,128]{5,3,4,2,1,0:T(8,128)(2,1)}, bf16[4,4,4,128,1,128]{5,3,4,2,1,0:T(8,128)(2,1)}) fusion(f32[4,4,128,128]{3,2,1,0:T(8,128)S(1)} %get-tuple-element.12, f32[4,4,128,128]{3,2,1,0:T(8,128)S(1)} %bitcast.237, f32[4,4,128,128]{3,2,1,0:T(8,128)S(1)} %get-tuple-element.11, f32[4,4,128,128]{3,2,1,0:T(8,128)S(1)} %bitcast.235), kind=kLoop, calls=%fused_computation.30 | loop fusion | flops 8388608 | bytes 8388608 | tf_op jit(solution)/shard_map/convert.7
  93.6 8.0 %fusion.3 = f32[2,128,4,4,4,128,1]{5,1,6,0,4,3,2:T(8,128)} fusion(bf16[4,4,4,128,1,128]{5,3,4,2,1,0:T(8,128)(2,1)} %get-tuple-element.8, bf16[4,4,4,128,1,128]{5,3,4,2,1,0:T(8,128)(2,1)} %get-tuple-element.7, bf16[1,128,2,128]{3,1,0,2:T(8,128)(2,1)S(1)} %get-tuple-element.16, bf16[1,128,2,128]{3,1,0,2:T(8,128)(2,1)S(1)} %get-tuple-element.15), kind=kOutput, calls=%fused_computation.8 | convolution fusion | flops 2158493696 | bytes 12713984 | tf_op jit(solution)/shard_map/ctxypz,pyqk->ctxkqz/dot_general | solution.py:46
  101.5 35.9 %all-to-all-done.1 = bf16[4,4,128,4,2,128]{5,3,1,0,4,2:T(4,128)(2,1)} async-done(((bf16[4,4,128,4,2,128]{5,3,1,0,4,2:T(4,128)(2,1)}), bf16[4,4,128,4,2,128]{5,3,1,0,4,2:T(4,128)(2,1)}, u32[]{:S(2)}, u32[]{:S(2)}) %all-to-all-start.1) | async-done | bytes 4194336 | tf_op jit(solution)/shard_map/all_to_all | solution.py:55
  137.4 7.6 %copy.67 = f32[4,4,32,4,4,2,128]{6,4,2,5,3,1,0:T(4,128)} copy(bf16[4,4,32,4,4,2,128]{6,4,1,0,5,3,2:T(4,128)(2,1)} %bitcast.90) | data formatting | bytes 12582912 | tf_op jit(solution)/shard_map/convert_element_type | solution.py:85
  145.0 11.5 %fusion.27 = f32[4,4,4,128,2,128]{5,3,4,2,1,0:T(8,128)} fusion(f32[4,4,4,128,2,128]{5,3,4,2,1,0:T(8,128)} %bitcast.234, f32[2,128,4,4,4,128,1]{5,1,6,0,4,3,2:T(8,128)} %fusion.3, f32[4,128,128]{2,1,0:T(8,128)S(1)} %bitcast.240, bf16[1,128,2,128]{3,1,2,0:T(8,128)(2,1)S(1)} %get-tuple-element.17, bf16[1,128,2,128]{3,1,2,0:T(8,128)(2,1)S(1)} %get-tuple-element.18), kind=kOutput, calls=%fused_computation.32 | convolution fusion | flops 2156396544 | bytes 25559040 | tf_op jit(solution)/shard_map/ctxypz,pzqk->ctxyqk/dot_general | solution.py:46
  156.5 4.3 %add_reduce_fusion = (f32[4,4,128,128]{3,2,1,0:T(8,128)S(1)}, f32[4,4,128,128]{3,2,1,0:T(8,128)S(1)}) fusion(f32[4,4,4,128,2,128]{5,3,4,2,1,0:T(8,128)} %fusion.27, f32[4,4,128,128]{3,2,1,0:T(8,128)S(1)} %bitcast.238, f32[4,4,128,128]{3,2,1,0:T(8,128)S(1)} %bitcast.236), kind=kLoop, calls=%fused_computation.28 | loop fusion | flops 7864320 | bytes 12582912 | tf_op jit(solution)/shard_map/reduce_sum | solution.py:92
  160.8 9.6 %fusion.45 = (f32[4,4,128,1,128]{4,0,3,2,1:T(4,128)S(1)}, f32[4,4,128,1,128]{4,0,3,2,1:T(4,128)S(1)}) fusion(f32[4,4,128,128]{3,2,1,0:T(8,128)S(1)} %get-tuple-element.6, f32[4,4,128,128]{3,2,1,0:T(8,128)S(1)} %get-tuple-element.5, s32[4]{0:T(128)S(1)} %copy-done.3, s32[4,128,128]{2,1,0:T(8,128)S(1)} %copy-done.1), kind=kLoop, calls=%fused_computation.58 | loop fusion | flops 5242880 | bytes 4456464 | tf_op jit(solution)/shard_map/add | solution.py:94
  170.5 8.0 %fusion.6 = bf16[16,4,128,2,128]{4,0,2,1,3:T(8,128)(2,1)S(1)} fusion(f32[4,4,128,1,128]{4,0,3,2,1:T(4,128)S(1)} %get-tuple-element.10, f32[4,4,128,1,128]{4,0,3,2,1:T(4,128)S(1)} %get-tuple-element.9, f32[4,1,16,2]{2,0,1,3:T(4,128)S(1)} %get-tuple-element.22, f32[4,1,16,2]{2,0,1,3:T(4,128)S(1)} %get-tuple-element.21), kind=kOutput, calls=%fused_computation.10 | convolution fusion | flops 203948288 | bytes 6292480 | tf_op jit(solution)/shard_map/txypz,tplq->lxyqz/dot_general | solution.py:99
  178.5 3.1 %copy.73 = bf16[16,4,128,2,128]{4,2,3,1,0:T(8,128)(2,1)} copy(bf16[16,4,128,2,128]{4,0,2,1,3:T(8,128)(2,1)S(1)} %fusion.6) | data formatting | bytes 8388608 | tf_op jit(solution)/shard_map/convert_element_type | solution.py:101
  181.5 0.0 reduce-scatter.2.cloned.1.call-update
  181.6 63.4 %reduce-scatter.2.cloned.1.call-done = bf16[2,4,128,2,128]{4,2,3,1,0:T(8,128)(2,1)} async-done(((bf16[16,4,128,2,128]{4,2,3,1,0:T(8,128)(2,1)}), bf16[2,4,128,2,128]{4,2,3,1,0:T(8,128)(2,1)}) %reduce-scatter.2.cloned.1.call-update) | async-done | bytes 524304 | tf_op jit(solution)/shard_map/reduce_scatter | solution.py:98
  245.0 2.6 %copy.74 = f32[2,4,128,2,128]{4,3,2,1,0:T(2,128)} copy(bf16[2,4,128,2,128]{4,2,3,1,0:T(8,128)(2,1)} %reduce-scatter.2.cloned.1.call-done) | data formatting | bytes 1572864 | tf_op jit(solution)/shard_map/convert_element_type | solution.py:105
  (10 shorter events, 0.1 us)
Async XLA Ops:
  6.5 74.2 %all-gather.2.cloned.1.call-start = ((), (), s32[]{:S(2)}) async-start(), calls=%async_computation.3 | async-start | bytes 4718592 | tf_op jit(solution)/shard_map/all_gather | solution.py:65
  9.9 23.7 %all-to-all-start = ((bf16[32,4,4,128]{3,2,1,0:T(4,128)(2,1)}), bf16[32,4,4,128]{3,2,1,0:T(4,128)(2,1)S(1)}, u32[]{:S(2)}, u32[]{:S(2)}) async-start(bf16[32,4,4,128]{3,2,1,0:T(4,128)(2,1)} %stack.76), calls=%async_computation | async-start | bytes 262144 | tf_op jit(solution)/shard_map/all_to_all | solution.py:57
  32.4 10.1 %copy-start.2 = (bf16[2,16,4]{1,2,0:T(4,128)(2,1)S(1)}, bf16[2,16,4]{1,2,0:T(4,128)(2,1)}, u32[]{:S(2)}) copy-start(bf16[2,16,4]{1,2,0:T(4,128)(2,1)} %param.7) | copy-start | bytes 772
  32.4 10.6 %copy-start = (bf16[4,4,128,2,128]{4,3,2,1,0:T(2,128)(2,1)S(1)}, bf16[4,4,128,2,128]{4,3,2,1,0:T(2,128)(2,1)}, u32[]{:S(2)}) copy-start(bf16[4,4,128,2,128]{4,3,2,1,0:T(2,128)(2,1)} %param.8) | copy-start | bytes 3145732
  33.6 103.8 %all-to-all-start.1 = ((bf16[4,4,128,4,2,128]{5,3,1,0,4,2:T(4,128)(2,1)}), bf16[4,4,128,4,2,128]{5,3,1,0,4,2:T(4,128)(2,1)}, u32[]{:S(2)}, u32[]{:S(2)}) async-start(bf16[4,4,128,4,2,128]{5,3,1,0,4,2:T(4,128)(2,1)} %copy.66), calls=%async_computation.1 | async-start | bytes 8388608 | tf_op jit(solution)/shard_map/all_to_all | solution.py:55
  42.4 202.5 %reduce-scatter.2.cloned.1.call-start = ((), (), s32[]{:S(2)}) async-start(), calls=%async_computation.4 | async-start | bytes 4718592 | tf_op jit(solution)/shard_map/reduce_scatter | solution.py:98
  80.7 5.1 %copy-start.1 = (s32[4,128,128]{2,1,0:T(8,128)S(1)}, s32[4,128,128]{2,1,0:T(8,128)}, u32[]{:S(2)}) copy-start(s32[4,128,128]{2,1,0:T(8,128)} %param.9) | copy-start | bytes 786436
  80.7 5.1 %copy-start.3 = (s32[4]{0:T(128)S(1)}, s32[4]{0:T(128)}, u32[]{:S(2)}) copy-start(s32[4]{0:T(128)} %iota_add_fusion) | copy-start | bytes 52
Sparse Core Ops, SparseCore 0:
  9.1 71.5 all-gather.1
  181.7 63.2 reduce-scatter.1
